TPU v7x, 256 devices: a whole 4x4x8 slice. The times are simulated.
256 devices in a mesh: wide: 32 (over x, y, core), narrow: 8 (over z).
Axes of the slice: x: 4, y: 4, z: 8, core: 2. Of those that a mesh axis runs over, the one named last changes fastest.
Arguments:
- momentum: float32 [9216, 9216], P('wide', 'narrow'), may hold values from -3 to 3
- gradient: bfloat16 [9216, 9216], P('wide', 'narrow'), may hold values from -48 to 48
- right_factor: float32 [512, 9216], P('wide', 'narrow'), may hold values from -6 to 6
Outputs:
- new_momentum: float32 [9216, 9216], P('wide', 'narrow')
- new_right: float32 [512, 9216], P('wide', 'narrow')
- update: bfloat16 [9216, 9216], P('wide', 'narrow')
All inputs are finite; a program needn't handle non-finite values.
Results may differ from a plain program's by a relative error of at most 0.001.
Values sent between devices are 32-bit elements; how exact they have to be, the bound alone decides.
A program may use at most 64 MiB of HBM per device.

v0:
```python
import functools
import jax
import jax.numpy as jnp
from jax import lax
from jax.experimental import pallas as pl
from jax.experimental.pallas import tpu as pltpu
from jax.sharding import Mesh
from jax.sharding import PartitionSpec as P

N_COLS = 9216
WIDE = ("wide_0", "wide_1", "wide_2")
EPS = 1e-06
MU = 0.95
MESH = pl.DeviceIdType.MESH
ROWS, COLS, RANK, STRIP, BLOCK = 288, 1152, 512, 40, 128
PAIRS = [(i, j) for i in range(4) for j in range(i + 1)]


def product(a, b, ca, cb):
    return lax.dot_general(a, b, (((ca,), (cb,)), ((), ())), preferred_element_type=jnp.float32)


def split(v):
    high = v.astype(jnp.bfloat16)
    return high, (v - high.astype(jnp.float32)).astype(jnp.bfloat16)


def dot_split(a, b, ca, cb):
    small = product(a[0], b[1], ca, cb) + product(a[1], b[0], ca, cb)
    return product(a[0], b[0], ca, cb) + small


def dot(a, b, ca, cb):
    return dot_split(split(a), split(b), ca, cb)


def dot_nt(a, b):
    return dot(a, b, 1, 1)


def dot_nn(a, b):
    return dot(a, b, 1, 0)


def lane_of(tile, lane):
    return jnp.broadcast_to(tile[:, lane:lane + 1], tile.shape)

def row_of(tile, row):
    return jnp.broadcast_to(tile[row:row + 1, :], tile.shape)

def inv_chol_block(d, hook):
    n = 128
    tiles = [d[8 * i:8 * i + 8, :] for i in range(n // 8)]
    lanes = lax.broadcasted_iota(jnp.int32, (8, n), 1)
    subs = lax.broadcasted_iota(jnp.int32, (8, n), 0)
    for j in range(n // 8):
        hook(j)
        t = tiles[j]
        inside = (lanes >= 8 * j) & (lanes < 8 * j + 8)
        cols = [lane_of(t, 8 * j + k) for k in range(8)]
        e = {(i, k): row_of(cols[k], i) for k in range(8) for i in range(k, 8)}
        raw = {i: [lane_of(tiles[i], 8 * j + k) for k in range(8)] for i in range(j + 1, n // 8)}
        own = jnp.where(inside, jnp.where(lanes - 8 * j == subs, 1.0, 0.0), t)
        rows = [row_of(own, k) for k in range(8)]
        scale, low = [], {}
        for k in range(8):
            scale.append(lax.rsqrt(e[k, k]))
            for i in range(k + 1, 8):
                low[i, k] = e[i, k] * scale[k]
            for i in range(k + 1, 8):
                for m in range(k + 1, i + 1):
                    e[i, m] = e[i, m] - low[i, k] * low[m, k]
        def forward(values):
            out = []
            for k in range(8):
                v = values[k]
                for m in range(k):
                    v = v - low[k, m] * out[m]
                out.append(v * scale[k])
            return out
        up = forward(rows)
        new = up[0]
        for k in range(1, 8):
            new = jnp.where(subs == k, up[k], new)
        tiles[j] = new
        for i in range(j + 1, n // 8):
            c = forward(raw[i])
            v = jnp.where(inside, 0.0, tiles[i])
            for k in range(8):
                v = v - c[k] * up[k]
            tiles[i] = v
    x = jnp.concatenate(tiles, axis=0)
    r = lax.broadcasted_iota(jnp.int32, (n, n), 0)
    c = lax.broadcasted_iota(jnp.int32, (n, n), 1)
    return jnp.where(c <= r, x, 0.0)

def inv_chol(m_ref, hooks, nb=4):
    b = 128
    for k in range(nb):
        s = slice(b * k, b * k + b)
        x = inv_chol_block(m_ref[s, s], lambda j: hooks.get((k, j), lambda: None)())
        if k:
            left = m_ref[s, :b * k]
            left = dot_nn(x, left)
            m_ref[s, :b * k] = left
        m_ref[s, s] = x
        for i in range(k + 1, nb):
            t = slice(b * i, b * i + b)
            c = dot_nt(m_ref[t, s], x)
            m_ref[t, s] = c
        for i in range(k + 1, nb):
            t = slice(b * i, b * i + b)
            c = m_ref[t, s]
            for q in range(k + 1, i + 1):
                u = slice(b * q, b * q + b)
                m_ref[t, u] = m_ref[t, u] - dot_nt(c, m_ref[u, s])
        for i in range(nb - 1, k, -1):
            t = slice(b * i, b * i + b)
            c = m_ref[t, s]
            if k:
                m_ref[t, :b * k] = m_ref[t, :b * k] - dot_nn(c, m_ref[s, :b * k])
            m_ref[t, s] = -dot_nn(c, x)
    for k in range(nb):
        for q in range(k + 1, nb):
            m_ref[b * k:b * k + b, b * q:b * q + b] = jnp.zeros((b, b), jnp.float32)


def step_kernel(
    momentum, gradient, right, new_momentum, new_right, update,
    mom, grad, a, a_h, a_l, r_all, part, z_got, p_all, g_part, g_comb, g_half, g_got, g_z, g_all, m,
    w_part, w_comb, w_half, w_got, w_all, s, p, q, n_z, roots,
    local, r_s, r_r, rf_s, rf_r, z_s, z_r, p_s, p_r, gc_s, gc_r, gr_s, gr_r, gz_s, gz_r, ga_s, ga_r, gf_s, gf_r,
    wc_s, wc_r, wr_s, wr_r, wa_s, wa_r, wf_s, wf_r, nz_s, nz_r,
):
    x, y, c, z = (lax.axis_index(n) for n in (*WIDE, "narrow"))
    xy = x * 4 + y
    sibling = (x, y, 1 - c, z)

    def plane(t):
        return (lax.rem(x + t // 4, 4), lax.rem(y + lax.rem(t, 4), 4), c, z)

    def plane_from(t):
        return lax.rem(x + 4 - t // 4, 4) * 4 + lax.rem(y + 4 - lax.rem(t, 4), 4)

    def column(t):
        return (x, y, c, lax.rem(z + t, 8))

    def column_from(t):
        return lax.rem(z + 8 - t, 8)

    def remote(src, dst, send, recv, to):
        return pltpu.make_async_remote_copy(
            src_ref=src, dst_ref=dst, send_sem=send, recv_sem=recv, device_id=to, device_id_type=MESH
        )

    pending = []

    def start_all(low, high, make):
        loop(low, high, lambda t: make(t).start())
        pending.append((low, high, make))

    def finish():
        for low, high, make in pending:
            loop(low, high, lambda t: make(t).wait_send())

    def loop(low, high, body):
        def run(i, carry):
            body(i)
            return carry

        lax.fori_loop(low, high, run, 0)

    loads = [
        pltpu.make_async_copy(right, r_all.at[x, y, c], local.at[0]),
        pltpu.make_async_copy(momentum, mom, local.at[1]),
        pltpu.make_async_copy(gradient, grad, local.at[2]),
    ]
    for load in loads:
        load.start()

    barrier = pltpu.get_barrier_semaphore()

    def hello(to):
        pl.semaphore_signal(barrier, inc=1, device_id=to, device_id_type=MESH)

    hello(sibling)
    loop(1, 16, lambda t: hello(plane(t)))
    loop(1, 8, lambda t: hello(column(t)))
    pl.semaphore_wait(barrier, 23)

    sense = 1 - 2 * c

    def wrap4(v):
        return lax.rem(v + 4, 4)

    def wrap8(v):
        return lax.rem(v + 8, 8)

    class PlaneGather:
        def __init__(self, piece, send, recv):
            self.piece, self.send, self.recv = piece, send, recv
            self.here = ((x, y), (y, x))

        def ref(self, h, u, v):
            return self.piece(h, u, v) if h == 0 else self.piece(h, v, u)

        def device(self, h, u, v):
            return (u, v, c, z) if h == 0 else (v, u, c, z)

        def go(self, h, index, origin, to):
            u, v = origin
            block = self.ref(h, wrap4(u), wrap4(v))
            i = 15 * h + index
            start_all(0, 1, lambda t: remote(
                block, block, self.send.at[i], self.recv.at[i], self.device(h, wrap4(to[0]), wrap4(to[1]))
            ))

        def come(self, h, index, origin):
            u, v = origin
            block = self.ref(h, wrap4(u), wrap4(v))
            i = 15 * h + index
            remote(block, block, self.send.at[i], self.recv.at[i], sibling).wait_recv()

        def origin(self, h, k):
            return self.here[h][0] + (0, -1, 1, 2)[k]

        def second(self, h, k):
            u0, v0 = self.here[h]
            u = self.origin(h, k)
            for j, hop in enumerate((2, 1, -1)):
                self.go(h, 3 + 3 * k + j, (u, v0), (u0, v0 + hop))

        def second_end(self, h, k):
            u, v0 = self.origin(h, k), self.here[h][1]
            for j, hop in enumerate((2, 1, -1)):
                self.come(h, 3 + 3 * k + j, (u, v0 - hop))

        def first(self):
            for j, hop in enumerate((2, 1, -1)):
                for h in range(2):
                    u0, v0 = self.here[h]
                    self.go(h, j, (u0, v0), (u0 + hop, v0))
            for h in range(2):
                self.second(h, 0)

        def middle(self):
            for k, j in ((1, 1), (2, 2), (3, 0)):
                for h in range(2):
                    self.come(h, j, (self.origin(h, k), self.here[h][1]))
                    self.second(h, k)

        def last(self, k):
            for h in range(2):
                self.second_end(h, k)

    def half_rows(h):
        return pl.ds(8 * h, 8)

    gather = PlaneGather(lambda h, xi, yi: r_all.at[xi, yi, c, half_rows(h)], r_s, r_r)

    def r_column(h, k, v):
        u = wrap4(gather.origin(h, k))
        return r_all.at[u, :, v, half_rows(h)] if h == 0 else r_all.at[:, u, v, half_rows(h)]

    def r_forward(h, k, v):
        block = r_column(h, k, v)
        return remote(block, block, rf_s.at[4 * h + k], rf_r.at[4 * h + k], sibling)

    def r_share(k):
        for h in range(2):
            start_all(0, 1, lambda t, h=h: r_forward(h, k, c))

    loads[0].wait()
    gather.first()
    loads[1].wait()
    loads[2].wait()
    a[...] = mom[...] + grad[...].astype(jnp.float32)
    a_h[...], a_l[...] = split(a[...])
    gather.middle()
    for k in range(4):
        gather.last(k)
        r_share(k)

    def z_rows(t):
        return pl.ds(pl.multiple_of(8 * ((9 * t) // 2), 8), STRIP)

    def z_target(d, n):
        return wrap8(z + (sense * (4 - n) if d == 0 else -sense * (3 - n)))

    def z_send(d, n, g):
        to = (x, y, c, wrap8(z + (sense if d == 0 else -sense)))
        src = part.at[g, z_rows(z_target(d, 0))] if n == 0 else z_got.at[d, n - 1, g]
        return remote(src, z_got.at[d, n, g], z_s.at[d, n, g], z_r.at[d, n, g], to)

    def z_wait(d, n, g):
        block = z_got.at[d, n, g]
        remote(block, block, z_s.at[d, n, g], z_r.at[d, n, g], sibling).wait_recv()

    for k in range(4):
        for h in range(2):
            r_forward(h, k, 1 - c).wait_recv()
    for g in range(4):
        ranks = split(r_all[g].reshape(BLOCK, COLS))
        part[g] = dot_split((a_h[...], a_l[...]), ranks, 1, 1)
        for d in range(2):
            start_all(0, 1, lambda t, d=d, g=g: z_send(d, 0, g))
    for n in range(1, 4):
        for g in range(4):
            for d in range(2):
                if d == 0 or n < 3:
                    z_wait(d, n - 1, g)
                    z_got[d, n - 1, g] = z_got[d, n - 1, g] + part[g, z_rows(z_target(d, n))]
                    start_all(0, 1, lambda t, d=d, n=n, g=g: z_send(d, n, g))
    total = []
    for g in range(4):
        z_wait(1, 2, g)
        z_wait(0, 3, g)
        total.append(part[g, z_rows(z)] + (z_got[0, 3, g] + z_got[1, 2, g]))
    for g in range(4):
        p_all[pl.ds(z, 1), g] = total[g].reshape(1, STRIP, BLOCK)

    def p_send(d, n, e):
        to = (x, y, c, wrap8(z + (sense if d == 0 else -sense)))
        block = p_all.at[wrap8(z - n * sense if d == 0 else z + n * sense), 2 * e : 2 * e + 2]
        return remote(block, block, p_s.at[d, n, e], p_r.at[d, n, e], to)

    def p_wait(d, n, e):
        block = p_all.at[wrap8(z - (n + 1) * sense if d == 0 else z + (n + 1) * sense), 2 * e : 2 * e + 2]
        remote(block, block, p_s.at[d, n, e], p_r.at[d, n, e], sibling).wait_recv()

    def p_step(n):
        for e in range(2):
            for d in range(2):
                if n > 0 and (d == 0 or n < 4):
                    p_wait(d, n - 1, e)
                if n < (4, 3)[d]:
                    start_all(0, 1, lambda t, d=d, e=e: p_send(d, n, e))

    p_step(0)

    tile_rows = lax.broadcasted_iota(jnp.int32, (STRIP, BLOCK), 0)
    fresh = (tile_rows >= 8) | (lax.rem(z, 2) == 0)
    own = [jnp.where(fresh, total[i], 0.0) for i in range(4)]
    pieces = []
    for i in range(4):
        wide = jnp.concatenate(own[: i + 1], axis=1)
        strip = dot(own[i], wide, 0, 0)
        pieces += [strip[:, BLOCK * j : BLOCK * j + BLOCK] for j in range(i + 1)]
    g_part[...] = jnp.concatenate(pieces, axis=0).reshape(16, 2, STRIP, BLOCK)

    p_step(1)
    g_swap = remote(g_part.at[:, 1 - c], g_comb, gc_s.at[0], gc_r.at[0], sibling)
    start_all(0, 1, lambda t: g_swap)
    g_swap.wait_recv()
    g_half[...] = g_part[:, pl.ds(c, 1)].reshape(16, STRIP, BLOCK) + g_comb[...]

    def g_send(t):
        tx, ty, _, _ = plane(t)
        return remote(g_half.at[tx * 4 + ty], g_got.at[t], gr_s.at[t], gr_r.at[t], plane(t))

    def g_wait(t):
        remote(g_got.at[t], g_got.at[t], gr_s.at[t], gr_r.at[t], plane(t)).wait_recv()

    start_all(1, 16, g_send)
    p_step(2)
    p_step(3)
    loop(1, 16, g_wait)
    strip = g_half[pl.ds(xy, 1)].reshape(STRIP, BLOCK)
    for t in range(1, 16):
        strip = strip + g_got[t]
    g_z[pl.ds(z, 1)] = strip.reshape(1, STRIP, BLOCK)

    def gz_send(t):
        return remote(g_z.at[z], g_z.at[z], gz_s.at[t], gz_r.at[t], column(t))

    def gz_wait(t):
        f = column_from(t)
        remote(g_z.at[f], g_z.at[f], gz_s.at[t], gz_r.at[t], column(t)).wait_recv()

    start_all(1, 8, gz_send)
    p_step(4)
    for t in range(8):
        first = (9 * t) // 2
        skip = t % 2
        for i in range(4):
            p[8 * (first + skip) : 8 * (first + 5), BLOCK * i : BLOCK * i + BLOCK] = p_all[t, i, 8 * skip :]
    for i in range(4):
        lanes = slice(BLOCK * i, BLOCK * i + BLOCK)
        w_part[4 * i : 4 * i + 4] = dot_split(split(p[:, lanes]), (a_h[...], a_l[...]), 0, 0).reshape(4, 2, 16, COLS)
    w_swap = remote(w_part.at[:, 1 - c], w_comb, wc_s.at[0], wc_r.at[0], sibling)
    start_all(0, 1, lambda t: w_swap)

    loop(1, 8, gz_wait)
    strip = g_z[0]
    for t in range(1, 8):
        strip = strip + g_z[t]
    g_all[pl.ds(xy, 1), pl.ds(c, 1)] = strip.reshape(1, 1, STRIP, BLOCK)

    def ga_send(t):
        return remote(g_all.at[xy, c], g_all.at[xy, c], ga_s.at[t], ga_r.at[t], plane(t))

    def ga_wait(t):
        f = plane_from(t)
        remote(g_all.at[f, c], g_all.at[f, c], ga_s.at[t], ga_r.at[t], plane(t)).wait_recv()

    start_all(1, 16, ga_send)

    w_swap.wait_recv()
    w_half[...] = w_part[:, pl.ds(c, 1)].reshape(16, 16, COLS) + w_comb[...]

    def w_send(t):
        tx, ty, _, _ = plane(t)
        return remote(w_half.at[tx * 4 + ty], w_got.at[t], wr_s.at[t], wr_r.at[t], plane(t))

    def w_wait(t):
        remote(w_got.at[t], w_got.at[t], wr_s.at[t], wr_r.at[t], plane(t)).wait_recv()

    start_all(1, 16, w_send)
    loop(1, 16, ga_wait)
    g_forward = remote(g_all.at[:, c], g_all.at[:, c], gf_s.at[0], gf_r.at[0], sibling)
    start_all(0, 1, lambda t: g_forward)

    remote(g_all.at[:, 1 - c], g_all.at[:, 1 - c], gf_s.at[0], gf_r.at[0], sibling).wait_recv()
    for n, (i, j) in enumerate(PAIRS):
        for k in range(16):
            t = 16 * n + k
            o, e = divmod(t, 5)
            m[BLOCK * i + 8 * k : BLOCK * i + 8 * k + 8, BLOCK * j : BLOCK * j + BLOCK] = g_all[
                o // 2, o % 2, 8 * e : 8 * e + 8
            ]

    w_gather = PlaneGather(lambda h, xi, yi: w_all.at[xi, yi, c, half_rows(h)], wa_s, wa_r)

    def w_own():
        loop(1, 16, w_wait)
        own = w_half[pl.ds(xy, 1)].reshape(16, COLS)
        for t in range(1, 16):
            own = own + w_got[t]
        w_all[pl.ds(x, 1), pl.ds(y, 1), pl.ds(c, 1)] = own.reshape(1, 1, 1, 16, COLS)

    def w_column(h, k, v):
        u = wrap4(w_gather.origin(h, k))
        block = w_all.at[u, :, v, half_rows(h)] if h == 0 else w_all.at[:, u, v, half_rows(h)]
        return remote(block, block, wf_s.at[4 * h + k], wf_r.at[4 * h + k], sibling)

    def w_share():
        for k in range(4):
            w_gather.last(k)
            for h in range(2):
                start_all(0, 1, lambda t, h=h, k=k: w_column(h, k, c))

    def w_first():
        w_own()
        w_gather.first()

    hooks = {WHEN[0]: w_first, WHEN[1]: w_gather.middle, WHEN[2]: w_share}
    inv_chol(m, hooks)

    for i in range(4):
        lanes = slice(BLOCK * i, BLOCK * i + BLOCK)
        q[:, lanes] = dot(p[:, : BLOCK * i + BLOCK], m[lanes, : BLOCK * i + BLOCK], 1, 1)
    for k in range(4):
        for h in range(2):
            w_column(h, k, 1 - c).wait_recv()
    squares = jnp.zeros((8, RANK), jnp.float32)
    ones = jnp.ones((8, COLS), jnp.float32)
    for i in range(4):
        rows = slice(BLOCK * i, BLOCK * i + BLOCK)
        known = w_all[: i + 1].reshape(BLOCK * i + BLOCK, COLS)
        block = dot(m[rows, : BLOCK * i + BLOCK], known, 1, 0)
        s[8 * i : 8 * i + 8] = block.reshape(8, 16, COLS)
        n_z[pl.ds(z, 1), :, rows] = dot(ones, block * block, 1, 1).reshape(1, 8, BLOCK)

    def nz_send(t):
        return remote(n_z.at[z], n_z.at[z], nz_s.at[t], nz_r.at[t], column(t))

    def nz_wait(t):
        f = column_from(t)
        remote(n_z.at[f], n_z.at[f], nz_s.at[t], nz_r.at[t], column(t)).wait_recv()

    start_all(1, 8, nz_send)
    sums = s[...].reshape(RANK, COLS)
    new_momentum[...] = a[...] - (1.0 - MU) * dot(q[...], sums, 1, 0)
    loop(1, 8, nz_wait)
    squares = n_z[0]
    for t in range(1, 8):
        squares = squares + n_z[t]
    root = jnp.sqrt(squares / N_COLS + EPS)
    update[...] = dot(q[...] * (1.0 / root[:1]), sums, 1, 0).astype(jnp.bfloat16)
    for i in range(4):
        turned = jnp.broadcast_to(root[:1, BLOCK * i : BLOCK * i + BLOCK], (BLOCK, BLOCK)).T
        roots[8 * i : 8 * i + 8] = turned.reshape(8, 16, BLOCK)
    mine = xy * 2 + c
    scale = roots[pl.ds(mine, 1)].reshape(16, BLOCK)
    strip = s[pl.ds(mine, 1)].reshape(16, COLS)
    for k in range(9):
        new_right[:, BLOCK * k : BLOCK * k + BLOCK] = strip[:, BLOCK * k : BLOCK * k + BLOCK] / scale

    finish()


WHEN = ((1, 4), (2, 4), (3, 6))


def per_device(momentum, gradient, right_factor):
    f32 = jnp.float32
    vmem, sem = pltpu.VMEM, pltpu.SemaphoreType.DMA
    scratch = [
        vmem((ROWS, COLS), f32), vmem((ROWS, COLS), jnp.bfloat16), vmem((ROWS, COLS), f32),
        vmem((ROWS, COLS), jnp.bfloat16), vmem((ROWS, COLS), jnp.bfloat16),
        vmem((4, 4, 2, 16, COLS), f32), vmem((4, ROWS, BLOCK), f32), vmem((2, 4, 4, STRIP, BLOCK), f32),
        vmem((8, 4, STRIP, BLOCK), f32),
        vmem((16, 2, STRIP, BLOCK), f32), vmem((16, STRIP, BLOCK), f32), vmem((16, STRIP, BLOCK), f32),
        vmem((16, STRIP, BLOCK), f32), vmem((8, STRIP, BLOCK), f32), vmem((16, 2, STRIP, BLOCK), f32),
        vmem((RANK, RANK), f32),
        vmem((16, 2, 16, COLS), f32), vmem((16, 16, COLS), f32), vmem((16, 16, COLS), f32),
        vmem((16, 16, COLS), f32), vmem((4, 4, 2, 16, COLS), f32),
        vmem((32, 16, COLS), f32),
        vmem((ROWS, RANK), f32), vmem((ROWS, RANK), f32), vmem((8, 8, RANK), f32), vmem((32, 16, BLOCK), f32),
        sem((3,)), sem((30,)), sem((30,)), sem((8,)), sem((8,)), sem((2, 4, 4)), sem((2, 4, 4)),
        sem((2, 4, 2)), sem((2, 4, 2)),
        sem((1,)), sem((1,)), sem((16,)), sem((16,)), sem((8,)), sem((8,)), sem((16,)), sem((16,)),
        sem((1,)), sem((1,)),
        sem((1,)), sem((1,)), sem((16,)), sem((16,)), sem((30,)), sem((30,)), sem((8,)), sem((8,)),
        sem((8,)), sem((8,)),
    ]
    return pl.pallas_call(
        step_kernel,
        out_shape=(
            jax.ShapeDtypeStruct((ROWS, COLS), f32),
            jax.ShapeDtypeStruct((16, COLS), f32),
            jax.ShapeDtypeStruct((ROWS, COLS), jnp.bfloat16),
        ),
        in_specs=[pl.BlockSpec(memory_space=pl.ANY)] * 3,
        out_specs=[pl.BlockSpec(memory_space=pltpu.VMEM)] * 3,
        scratch_shapes=scratch,
        compiler_params=pltpu.CompilerParams(
            collective_id=0, has_side_effects=True, vmem_limit_bytes=60 << 20
        ),
    )(momentum, gradient, right_factor)


def solution(mesh):
    finer = Mesh(
        mesh.devices.reshape(4, 4, 2, mesh.shape["narrow"]),
        ("wide_0", "wide_1", "wide_2", "narrow"),
    )
    return jax.shard_map(
        per_device,
        mesh=finer,
        in_specs=(P(WIDE, "narrow"), P(WIDE, "narrow"), P(WIDE, "narrow")),
        out_specs=(P(WIDE, "narrow"), P(WIDE, "narrow"), P(WIDE, "narrow")),
        check_vma=False,
    )
```

profile of v0, /device:TPU:1, one launch (start us, length us, event | category | flops | bytes accessed | tf_op | source)
XLA Modules:
  0.0 112.6 jit_solution(14281129321596870352)
XLA Ops:
  0.6 108.0 %shard_map.58 = (f32[288,1152]{1,0:T(8,128)}, f32[16,1152]{1,0:T(8,128)}, bf16[288,1152]{1,0:T(8,128)(2,1)}) custom-call(f32[288,1152]{1,0:T(8,128)} %momentum.1, bf16[288,1152]{1,0:T(8,128)(2,1)} %gradient.1, f32[16,1152]{1,0:T(8,128)} %right.1), custom_call_target="tpu_custom_call" | custom-call | tf_op jit(solution)/shard_map/pallas_call | solution.py:527
  108.6 0.0 copy-start.1
  108.6 0.0 copy-start
  108.6 2.5 %copy.9 = f32[288,1152]{1,0:T(8,128)} copy(f32[288,1152]{1,0:T(8,128)} %get-tuple-element.6) | data formatting | bytes 2654208
  111.2 0.0 copy-done.1
  111.2 0.6 copy.10
  111.8 0.0 copy-done
  111.8 0.8 copy.11
Async XLA Ops:
  108.6 2.6 %copy-start.1 = (f32[16,1152]{1,0:T(8,128)S(1)}, f32[16,1152]{1,0:T(8,128)}, u32[]{:S(2)}) copy-start(f32[16,1152]{1,0:T(8,128)} %get-tuple-element.7) | copy-start | bytes 221188
  108.6 3.2 %copy-start = (bf16[288,1152]{1,0:T(8,128)(2,1)S(1)}, bf16[288,1152]{1,0:T(8,128)(2,1)}, u32[]{:S(2)}) copy-start(bf16[288,1152]{1,0:T(8,128)(2,1)} %get-tuple-element.8) | copy-start | bytes 1990660
where the time goes:
time: 113 us
  Pallas kernels  108 us (96%)
  local copies, waits for them, and re-layouts  4.02 us (4%)
    pallas_call x1, Pallas kernels, per_device(): pl.pallas_call(step_kernel, out_shape=(jax.ShapeDtypeStruct((ROWS, COLS),...  108 us
    unnamed x7, local copies, waits for them, and re-layouts  4.02 us

commit v1 on v0

--- a/solution.py
+++ b/solution.py
@@ -128,7 +128,7 @@
 def step_kernel(
     momentum, gradient, right, new_momentum, new_right, update,
     mom, grad, a, a_h, a_l, r_all, part, z_got, p_all, g_part, g_comb, g_half, g_got, g_z, g_all, m,
-    w_part, w_comb, w_half, w_got, w_all, s, p, q, n_z, roots,
+    w_part, w_comb, w_half, w_got, w_h, w_l, w_all, s, p, q, n_z, roots,
     local, r_s, r_r, rf_s, rf_r, z_s, z_r, p_s, p_r, gc_s, gc_r, gr_s, gr_r, gz_s, gz_r, ga_s, ga_r, gf_s, gf_r,
     wc_s, wc_r, wr_s, wr_r, wa_s, wa_r, wf_s, wf_r, nz_s, nz_r,
 ):
@@ -462,14 +462,17 @@
     for k in range(4):
         for h in range(2):
             w_column(h, k, 1 - c).wait_recv()
-    squares = jnp.zeros((8, RANK), jnp.float32)
-    ones = jnp.ones((8, COLS), jnp.float32)
+    ones = jnp.ones((8, BLOCK), jnp.float32)
     for i in range(4):
-        rows = slice(BLOCK * i, BLOCK * i + BLOCK)
-        known = w_all[: i + 1].reshape(BLOCK * i + BLOCK, COLS)
-        block = dot(m[rows, : BLOCK * i + BLOCK], known, 1, 0)
+        rows, known = slice(BLOCK * i, BLOCK * i + BLOCK), slice(0, BLOCK * i + BLOCK)
+        w_h[rows], w_l[rows] = split(w_all[i].reshape(BLOCK, COLS))
+        block = dot_split(split(m[rows, known]), (w_h[known], w_l[known]), 1, 0)
         s[8 * i : 8 * i + 8] = block.reshape(8, 16, COLS)
-        n_z[pl.ds(z, 1), :, rows] = dot(ones, block * block, 1, 1).reshape(1, 8, BLOCK)
+        square = block * block
+        folded = square[:, :BLOCK]
+        for k in range(1, 9):
+            folded = folded + square[:, BLOCK * k : BLOCK * k + BLOCK]
+        n_z[pl.ds(z, 1), :, rows] = dot(ones, folded, 1, 1).reshape(1, 8, BLOCK)
 
     def nz_send(t):
         return remote(n_z.at[z], n_z.at[z], nz_s.at[t], nz_r.at[t], column(t))
@@ -479,14 +482,14 @@
         remote(n_z.at[f], n_z.at[f], nz_s.at[t], nz_r.at[t], column(t)).wait_recv()
 
     start_all(1, 8, nz_send)
-    sums = s[...].reshape(RANK, COLS)
-    new_momentum[...] = a[...] - (1.0 - MU) * dot(q[...], sums, 1, 0)
+    w_h[...], w_l[...] = split(s[...].reshape(RANK, COLS))
+    new_momentum[...] = a[...] - (1.0 - MU) * dot_split(split(q[...]), (w_h[...], w_l[...]), 1, 0)
     loop(1, 8, nz_wait)
     squares = n_z[0]
     for t in range(1, 8):
         squares = squares + n_z[t]
     root = jnp.sqrt(squares / N_COLS + EPS)
-    update[...] = dot(q[...] * (1.0 / root[:1]), sums, 1, 0).astype(jnp.bfloat16)
+    update[...] = dot_split(split(q[...] * (1.0 / root[:1])), (w_h[...], w_l[...]), 1, 0).astype(jnp.bfloat16)
     for i in range(4):
         turned = jnp.broadcast_to(root[:1, BLOCK * i : BLOCK * i + BLOCK], (BLOCK, BLOCK)).T
         roots[8 * i : 8 * i + 8] = turned.reshape(8, 16, BLOCK)
@@ -514,7 +517,8 @@
         vmem((16, STRIP, BLOCK), f32), vmem((8, STRIP, BLOCK), f32), vmem((16, 2, STRIP, BLOCK), f32),
         vmem((RANK, RANK), f32),
         vmem((16, 2, 16, COLS), f32), vmem((16, 16, COLS), f32), vmem((16, 16, COLS), f32),
-        vmem((16, 16, COLS), f32), vmem((4, 4, 2, 16, COLS), f32),
+        vmem((16, 16, COLS), f32),
+        vmem((RANK, COLS), jnp.bfloat16), vmem((RANK, COLS), jnp.bfloat16), vmem((4, 4, 2, 16, COLS), f32),
         vmem((32, 16, COLS), f32),
         vmem((ROWS, RANK), f32), vmem((ROWS, RANK), f32), vmem((8, 8, RANK), f32), vmem((32, 16, BLOCK), f32),
         sem((3,)), sem((30,)), sem((30,)), sem((8,)), sem((8,)), sem((2, 4, 4)), sem((2, 4, 4)),

time: 113 us -> 112 us (level)
  no operation moved by 1% of the time
where the time goes in v1:
time: 112 us
  Pallas kernels  107 us (96%)
  local copies, waits for them, and re-layouts  4.02 us (4%)
    pallas_call x1, Pallas kernels, per_device(): pl.pallas_call(step_kernel, out_shape=(jax.ShapeDtypeStruct((ROWS, COLS),...  107 us
    unnamed x7, local copies, waits for them, and re-layouts  4.02 us

profile of v1, /device:TPU:1, one launch (start us, length us, event | category | flops | bytes accessed | tf_op | source)
XLA Modules:
  0.0 112.1 jit_solution(15647050517715998810)
XLA Ops:
  0.6 107.5 %shard_map.58 = (f32[288,1152]{1,0:T(8,128)}, f32[16,1152]{1,0:T(8,128)}, bf16[288,1152]{1,0:T(8,128)(2,1)}) custom-call(f32[288,1152]{1,0:T(8,128)} %momentum.1, bf16[288,1152]{1,0:T(8,128)(2,1)} %gradient.1, f32[16,1152]{1,0:T(8,128)} %right.1), custom_call_target="tpu_custom_call" | custom-call | tf_op jit(solution)/shard_map/pallas_call | solution.py:531
  108.1 0.0 copy-start.1
  108.1 0.0 copy-start
  108.1 2.5 %copy.9 = f32[288,1152]{1,0:T(8,128)} copy(f32[288,1152]{1,0:T(8,128)} %get-tuple-element.6) | data formatting | bytes 2654208
  110.7 0.0 copy-done.1
  110.7 0.6 copy.10
  111.3 0.0 copy-done
  111.3 0.8 copy.11
Async XLA Ops:
  108.1 2.6 %copy-start.1 = (f32[16,1152]{1,0:T(8,128)S(1)}, f32[16,1152]{1,0:T(8,128)}, u32[]{:S(2)}) copy-start(f32[16,1152]{1,0:T(8,128)} %get-tuple-element.7) | copy-start | bytes 221188
  108.1 3.2 %copy-start = (bf16[288,1152]{1,0:T(8,128)(2,1)S(1)}, bf16[288,1152]{1,0:T(8,128)(2,1)}, u32[]{:S(2)}) copy-start(bf16[288,1152]{1,0:T(8,128)(2,1)} %get-tuple-element.8) | copy-start | bytes 1990660
